TPU v7x, 32 devices: a whole 2x2x4 slice. The times are simulated.
32 devices in a mesh: rep: 4 (over y, core), shard: 4 (over z), ctx: 2 (over x).
Axes of the slice: x: 2, y: 2, z: 4, core: 2. Of those that a mesh axis runs over, the one named last changes fastest.
Arguments:
- tokens: bfloat16 [2, 4, 512, 2048], P(None, 'rep', ('shard', 'ctx')), may hold values from -6 to 6
- span_starts: int32 [2, 4], P(None, 'rep'), may hold values from 0 to 256
- cotangent: bfloat16 [2, 4, 512, 2048], P(None, 'rep', ('shard', 'ctx')), may hold values from -6 to 6
- w_query: bfloat16 [2048, 2048], P('shard'), may hold values from -0.125 to 0.125
- key_weight: bfloat16 [2048, 1024], P('shard'), may hold values from -0.125 to 0.125
- value_weight: bfloat16 [2048, 1024], P('shard'), may hold values from -0.125 to 0.125
- w_out: bfloat16 [2048, 2048], P('shard'), may hold values from -0.75 to 0.75
- attn_gain: bfloat16 [2048], P('shard'), may hold values from 0.099609375 to 1.8984375
- query_gain: bfloat16 [128], P('shard'), may hold values from 0.099609375 to 1.8984375
- key_gain: bfloat16 [128], P('shard'), may hold values from 0.099609375 to 1.8984375
- w_gate: bfloat16 [2048, 6144], P('shard'), may hold values from -0.125 to 0.125
- w_up: bfloat16 [2048, 6144], P('shard'), may hold values from -0.125 to 0.125
- w_down: bfloat16 [6144, 2048], P('shard'), may hold values from -0.078125 to 0.078125
- ffn_gain: bfloat16 [2048], P('shard'), may hold values from 0.099609375 to 1.8984375
Outputs:
- output: bfloat16 [2, 4, 512, 2048], P(None, 'rep', ('shard', 'ctx'))
- input_grad: float32 [2, 4, 512, 2048], P(None, 'rep', ('shard', 'ctx'))
- grad_query: float32 [2048, 2048], P('shard')
- grad_key: float32 [2048, 1024], P('shard')
- grad_value: float32 [2048, 1024], P('shard')
- grad_out: float32 [2048, 2048], P('shard')
- grad_attn_gain: float32 [2048], P('shard')
- grad_query_gain: float32 [128], P('shard')
- grad_key_gain: float32 [128], P('shard')
- grad_gate: float32 [2048, 6144], P('shard')
- grad_up: float32 [2048, 6144], P('shard')
- grad_down: float32 [6144, 2048], P('shard')
- grad_ffn_gain: float32 [2048], P('shard')
Inputs may be any that keep to these rules, and one draw needn't show every extreme that they name: `span_starts`: each sequence's picture span covers positions start to start + 255 of that sequence.
All inputs are finite; a program needn't handle non-finite values.
Results may differ from a plain program's by a relative error of at most 0.023.
Values may be sent and summed in bfloat16 or wider, within the bound.
No kernel may reach another device: no remote copies, remote signals or barrier semaphores. Data moves between devices by JAX's collectives and lax.ppermute only.
A program may use at most 448 MiB of HBM per device.

v0:
```python
from functools import partial
import jax
import jax.numpy as jnp
from jax import lax
from jax.sharding import PartitionSpec as P

QUERY_HEADS = 16
KEY_VALUE_HEADS = 8
HEAD_SIZE = 128
PIC = 256
EPSILON = 1e-06
THETA = 1000000.0


def apply_rotation(values):
    half_width = values.shape[-1] // 2
    return jnp.concatenate([-values[..., half_width:], values[..., :half_width]], axis=-1)


def rotate_back(values):
    half_width = values.shape[-1] // 2
    return jnp.concatenate([values[..., half_width:], -values[..., :half_width]], axis=-1)


def spin_tables(positions):
    inverse = THETA ** (-jnp.arange(HEAD_SIZE // 2, dtype=jnp.float32) * 2.0 / HEAD_SIZE)
    angles = positions.astype(jnp.float32)[:, None] * inverse[None, :]
    cosine_table = jnp.concatenate([jnp.cos(angles), jnp.cos(angles)], axis=-1)[:, None, :]
    sine_values = jnp.concatenate([jnp.sin(angles), jnp.sin(angles)], axis=-1)[:, None, :]
    return (cosine_table, sine_values)


def recip_rms(values):
    return lax.rsqrt(jnp.mean(values * values, axis=-1, keepdims=True) + EPSILON)


def norm_back(unit, recip, gain, d_normed):
    d_unit = d_normed * gain
    return recip * (d_unit - unit * jnp.mean(d_unit * unit, axis=-1, keepdims=True))


def over_rows(left, right):
    return lax.dot_general(
        left, right, (((0,), (0,)), ((), ())), preferred_element_type=jnp.float32
    )


def compared_to(left, right):
    return lax.dot_general(
        left, right, (((1,), (1,)), ((), ())), preferred_element_type=jnp.float32
    )


def attention_set(w_query, key_weight, value_weight, w_out, attn_gain, query_gain, key_gain):
    return (
        lax.all_gather(w_query, "shard", axis=0, tiled=True),
        lax.all_gather(key_weight, "shard", axis=0, tiled=True),
        lax.all_gather(value_weight, "shard", axis=0, tiled=True),
        lax.all_gather(w_out, "shard", axis=0, tiled=True),
        lax.all_gather(attn_gain, "shard", axis=0, tiled=True),
        lax.all_gather(query_gain, "shard", axis=0, tiled=True),
        lax.all_gather(key_gain, "shard", axis=0, tiled=True),
    )


def feedforward_set(w_gate, w_up, w_down, ffn_gain):
    return (
        lax.all_gather(w_gate, "shard", axis=0, tiled=True),
        lax.all_gather(w_up, "shard", axis=0, tiled=True),
        lax.all_gather(w_down, "shard", axis=0, tiled=True),
        lax.all_gather(ffn_gain, "shard", axis=0, tiled=True),
    )


def masked_scores(allowed, q_head, k_head):
    scores = jnp.einsum(
        "tgd,sd->gts", q_head, k_head, preferred_element_type=jnp.float32
    ) * HEAD_SIZE ** (-0.5)
    return jnp.where(allowed, scores, -1e30)


def head_forward(allowed, pieces):
    q_head, k_head, v_head = pieces
    scores = masked_scores(allowed, q_head, k_head)
    highest = jnp.max(scores, axis=-1, keepdims=True)
    log_total = highest + jnp.log(jnp.sum(jnp.exp(scores - highest), axis=-1, keepdims=True))
    probs_low = jnp.exp(scores - log_total).astype(jnp.bfloat16)
    mixed = jnp.einsum("gts,sd->tgd", probs_low, v_head, preferred_element_type=jnp.float32)
    return (mixed, log_total)


def head_backward(allowed, pieces):
    q_head, k_head, v_head, d_mix_head, log_total = pieces
    probs = jnp.exp(masked_scores(allowed, q_head, k_head) - log_total)
    probs_low = probs.astype(jnp.bfloat16)
    d_probs = jnp.einsum("tgd,sd->gts", d_mix_head, v_head, preferred_element_type=jnp.float32)
    d_values = jnp.einsum("gts,tgd->sd", probs_low, d_mix_head, preferred_element_type=jnp.float32)
    row_dot = jnp.sum(probs * d_probs, axis=-1, keepdims=True)
    d_scores = (probs * (d_probs - row_dot)).astype(jnp.bfloat16)
    d_queries = jnp.einsum(
        "gts,sd->tgd", d_scores, k_head, preferred_element_type=jnp.float32
    ) * HEAD_SIZE ** (-0.5)
    d_keys = jnp.einsum(
        "gts,tgd->sd", d_scores, q_head, preferred_element_type=jnp.float32
    ) * HEAD_SIZE ** (-0.5)
    return (d_queries, d_keys, d_values)


def shards(
    tokens,
    span_starts,
    cotangent,
    w_query,
    key_weight,
    value_weight,
    w_out,
    attn_gain,
    query_gain,
    key_gain,
    w_gate,
    w_up,
    w_down,
    ffn_gain,
):
    seq_count = lax.axis_size(("shard", "ctx"))
    seq_rank = lax.axis_index(("shard", "ctx"))
    token_rows = tokens.shape[2]
    token_length = token_rows * seq_count
    group_width = QUERY_HEADS // KEY_VALUE_HEADS
    local_pos = seq_rank * token_rows + jnp.arange(token_rows, dtype=jnp.int32)
    key_pos = jnp.arange(token_length, dtype=jnp.int32)
    cosine_table, sine_values = spin_tables(local_pos)
    cos_keys = cosine_table[:, 0, :][None]
    sin_keys = sine_values[:, 0, :][None]
    out_list = []
    grad_list = []
    stored = []
    totals = None
    for micro_index in range(tokens.shape[0]):
        span_start = span_starts[micro_index, 0]
        inside_q = (local_pos >= span_start) & (local_pos < span_start + PIC)
        inside_k = (key_pos >= span_start) & (key_pos < span_start + PIC)
        allowed = (key_pos[None, :] <= local_pos[:, None]) | inside_q[:, None] & inside_k[None, :]
        hidden_in = tokens[micro_index, 0].astype(jnp.float32)
        full_query, full_key, full_value, complete_output, gain_attn, gain_query, gain_key = (
            attention_set(w_query, key_weight, value_weight, w_out, attn_gain, query_gain, key_gain)
        )
        gain_attn = gain_attn.astype(jnp.float32)
        gain_query = gain_query.astype(jnp.float32)
        gain_key = gain_key.astype(jnp.float32)
        recip_h = recip_rms(hidden_in)
        unit_h = hidden_in * recip_h
        normalized_rows = (unit_h * gain_attn).astype(jnp.bfloat16)
        q_pre = jnp.dot(normalized_rows, full_query, preferred_element_type=jnp.float32).reshape(
            token_rows, QUERY_HEADS, HEAD_SIZE
        )
        key_before_rotation = jnp.transpose(
            jnp.dot(normalized_rows, full_key, preferred_element_type=jnp.float32).reshape(
                token_rows, KEY_VALUE_HEADS, HEAD_SIZE
            ),
            (1, 0, 2),
        )
        value_local = jnp.transpose(
            jnp.dot(normalized_rows, full_value, preferred_element_type=jnp.float32)
            .astype(jnp.bfloat16)
            .reshape(token_rows, KEY_VALUE_HEADS, HEAD_SIZE),
            (1, 0, 2),
        )
        recip_q = recip_rms(q_pre)
        unit_query = q_pre * recip_q
        recip_k = recip_rms(key_before_rotation)
        unit_k = key_before_rotation * recip_k
        scaled_q = unit_query * gain_query
        scaled_k = unit_k * gain_key
        query_rows = jnp.transpose(
            (scaled_q * cosine_table + apply_rotation(scaled_q) * sine_values)
            .astype(jnp.bfloat16)
            .reshape(token_rows, KEY_VALUE_HEADS, group_width, HEAD_SIZE),
            (1, 0, 2, 3),
        )
        key_local = (scaled_k * cos_keys + apply_rotation(scaled_k) * sin_keys).astype(jnp.bfloat16)
        key_rows, value_matrix = (
            lax.all_gather(key_local, ("shard", "ctx"), axis=1, tiled=True),
            lax.all_gather(value_local, ("shard", "ctx"), axis=1, tiled=True),
        )
        mixed_split, log_total = lax.map(
            partial(head_forward, allowed), (query_rows, key_rows, value_matrix)
        )
        mixed_heads = (
            jnp.transpose(mixed_split, (1, 0, 2, 3))
            .reshape(token_rows, QUERY_HEADS * HEAD_SIZE)
            .astype(jnp.bfloat16)
        )
        middle = hidden_in + jnp.dot(
            mixed_heads, complete_output, preferred_element_type=jnp.float32
        )
        full_gate, full_up, full_down, gain_ffn = feedforward_set(w_gate, w_up, w_down, ffn_gain)
        gain_ffn = gain_ffn.astype(jnp.float32)
        recip_m = recip_rms(middle)
        unit_m = middle * recip_m
        ffn_in = (unit_m * gain_ffn).astype(jnp.bfloat16)
        gate_pre = jnp.dot(ffn_in, full_gate, preferred_element_type=jnp.float32)
        up_pre = jnp.dot(ffn_in, full_up, preferred_element_type=jnp.float32)
        sigma = jax.nn.sigmoid(gate_pre)
        act_gate = gate_pre * sigma
        inner_act = (act_gate * up_pre).astype(jnp.bfloat16)
        result = middle + jnp.dot(inner_act, full_down, preferred_element_type=jnp.float32)
        out_list.append(result.astype(jnp.bfloat16))
        cot_rows = cotangent[micro_index, 0]
        cot_float = cot_rows.astype(jnp.float32)
        d_inner = compared_to(cot_rows, full_down)
        d_gate = (d_inner * up_pre * sigma * (1.0 + gate_pre * (1.0 - sigma))).astype(jnp.bfloat16)
        d_up = (d_inner * act_gate).astype(jnp.bfloat16)
        d_ffn_in = compared_to(d_gate, full_gate) + compared_to(d_up, full_up)
        ffn_gain_part = jnp.sum(d_ffn_in * unit_m, axis=0)
        d_middle = cot_float + norm_back(unit_m, recip_m, gain_ffn, d_ffn_in)
        branch_gradient = d_middle.astype(jnp.bfloat16)
        d_mixed = jnp.transpose(
            compared_to(branch_gradient, complete_output)
            .astype(jnp.bfloat16)
            .reshape(token_rows, KEY_VALUE_HEADS, group_width, HEAD_SIZE),
            (1, 0, 2, 3),
        )
        d_split_q, d_keys, d_values = lax.map(
            partial(head_backward, allowed),
            (query_rows, key_rows, value_matrix, d_mixed, log_total),
        )
        d_queries = jnp.transpose(d_split_q, (1, 0, 2, 3)).reshape(
            token_rows, QUERY_HEADS, HEAD_SIZE
        )
        d_key_local, d_value_local = (
            lax.psum_scatter(
                d_keys.astype(jnp.bfloat16), ("shard", "ctx"), scatter_dimension=1, tiled=True
            ).astype(jnp.float32),
            lax.psum_scatter(
                d_values.astype(jnp.bfloat16), ("shard", "ctx"), scatter_dimension=1, tiled=True
            ).astype(jnp.float32),
        )
        d_unit_q = d_queries * cosine_table + rotate_back(d_queries * sine_values)
        d_unit_k = d_key_local * cos_keys + rotate_back(d_key_local * sin_keys)
        query_gain_part = jnp.sum(d_unit_q * unit_query, axis=(0, 1))
        key_gain_part = jnp.sum(d_unit_k * unit_k, axis=(0, 1))
        d_q_pre = (
            norm_back(unit_query, recip_q, gain_query, d_unit_q)
            .astype(jnp.bfloat16)
            .reshape(token_rows, QUERY_HEADS * HEAD_SIZE)
        )
        d_k_pre = jnp.transpose(
            norm_back(unit_k, recip_k, gain_key, d_unit_k).astype(jnp.bfloat16), (1, 0, 2)
        ).reshape(token_rows, KEY_VALUE_HEADS * HEAD_SIZE)
        d_v_pre = jnp.transpose(d_value_local.astype(jnp.bfloat16), (1, 0, 2)).reshape(
            token_rows, KEY_VALUE_HEADS * HEAD_SIZE
        )
        d_normed = (
            compared_to(d_q_pre, full_query)
            + compared_to(d_k_pre, full_key)
            + compared_to(d_v_pre, full_value)
        )
        attn_gain_part = jnp.sum(d_normed * unit_h, axis=0)
        grad_list.append(d_middle + norm_back(unit_h, recip_h, gain_attn, d_normed))
        stored.append(
            (
                normalized_rows,
                d_q_pre,
                d_k_pre,
                d_v_pre,
                mixed_heads,
                branch_gradient,
                ffn_in,
                d_gate,
                d_up,
                inner_act,
                cot_rows,
            )
        )
        parts = (attn_gain_part, query_gain_part, key_gain_part, ffn_gain_part)
        if totals is None:
            totals = parts
        else:
            totals = tuple((older + newer for older, newer in zip(totals, parts)))
    joined = [
        jnp.concatenate([saved_set[member] for saved_set in stored], axis=0) for member in range(11)
    ]
    (
        normed_all,
        dq_all,
        dk_all,
        dv_all,
        mixed_all,
        branch_all,
        ffn_all,
        gate_all,
        up_all,
        inner_all,
        cot_all,
    ) = joined
    totals = (
        lax.psum_scatter(
            over_rows(normed_all, dq_all).astype(jnp.bfloat16),
            "shard",
            scatter_dimension=0,
            tiled=True,
        ).astype(jnp.float32),
        lax.psum_scatter(
            over_rows(normed_all, dk_all).astype(jnp.bfloat16),
            "shard",
            scatter_dimension=0,
            tiled=True,
        ).astype(jnp.float32),
        lax.psum_scatter(
            over_rows(normed_all, dv_all).astype(jnp.bfloat16),
            "shard",
            scatter_dimension=0,
            tiled=True,
        ).astype(jnp.float32),
        lax.psum_scatter(
            over_rows(mixed_all, branch_all).astype(jnp.bfloat16),
            "shard",
            scatter_dimension=0,
            tiled=True,
        ).astype(jnp.float32),
        lax.psum_scatter(
            totals[0].astype(jnp.bfloat16), "shard", scatter_dimension=0, tiled=True
        ).astype(jnp.float32),
        lax.psum_scatter(
            totals[1].astype(jnp.bfloat16), "shard", scatter_dimension=0, tiled=True
        ).astype(jnp.float32),
        lax.psum_scatter(
            totals[2].astype(jnp.bfloat16), "shard", scatter_dimension=0, tiled=True
        ).astype(jnp.float32),
        lax.psum_scatter(
            over_rows(ffn_all, gate_all).astype(jnp.bfloat16),
            "shard",
            scatter_dimension=0,
            tiled=True,
        ).astype(jnp.float32),
        lax.psum_scatter(
            over_rows(ffn_all, up_all).astype(jnp.bfloat16),
            "shard",
            scatter_dimension=0,
            tiled=True,
        ).astype(jnp.float32),
        lax.psum_scatter(
            over_rows(inner_all, cot_all).astype(jnp.bfloat16),
            "shard",
            scatter_dimension=0,
            tiled=True,
        ).astype(jnp.float32),
        lax.psum_scatter(
            totals[3].astype(jnp.bfloat16), "shard", scatter_dimension=0, tiled=True
        ).astype(jnp.float32),
    )
    summed = (
        lax.psum(totals[0].astype(jnp.bfloat16), ("rep", "ctx")).astype(jnp.float32),
        lax.psum(totals[1].astype(jnp.bfloat16), ("rep", "ctx")).astype(jnp.float32),
        lax.psum(totals[2].astype(jnp.bfloat16), ("rep", "ctx")).astype(jnp.float32),
        lax.psum(totals[3].astype(jnp.bfloat16), ("rep", "ctx")).astype(jnp.float32),
        lax.psum(totals[4].astype(jnp.bfloat16), ("rep", "ctx")).astype(jnp.float32),
        lax.psum(totals[5].astype(jnp.bfloat16), ("rep", "ctx")).astype(jnp.float32),
        lax.psum(totals[6].astype(jnp.bfloat16), ("rep", "ctx")).astype(jnp.float32),
        lax.psum(totals[7].astype(jnp.bfloat16), ("rep", "ctx")).astype(jnp.float32),
        lax.psum(totals[8].astype(jnp.bfloat16), ("rep", "ctx")).astype(jnp.float32),
        lax.psum(totals[9].astype(jnp.bfloat16), ("rep", "ctx")).astype(jnp.float32),
        lax.psum(totals[10].astype(jnp.bfloat16), ("rep", "ctx")).astype(jnp.float32),
    )
    output = jnp.stack(out_list)[:, None]
    input_grad = jnp.stack(grad_list)[:, None]
    return (
        output,
        input_grad,
        summed[0],
        summed[1],
        summed[2],
        summed[3],
        summed[4],
        summed[5],
        summed[6],
        summed[7],
        summed[8],
        summed[9],
        summed[10],
    )


def solution(mesh):
    in_specs = (
        P(None, "rep", ("shard", "ctx"), None),
        P(None, "rep"),
        P(None, "rep", ("shard", "ctx"), None),
        P("shard", None),
        P("shard", None),
        P("shard", None),
        P("shard", None),
        P("shard"),
        P("shard"),
        P("shard"),
        P("shard", None),
        P("shard", None),
        P("shard", None),
        P("shard"),
    )
    out_specs = (
        P(None, "rep", ("shard", "ctx"), None),
        P(None, "rep", ("shard", "ctx"), None),
        P("shard", None),
        P("shard", None),
        P("shard", None),
        P("shard", None),
        P("shard"),
        P("shard"),
        P("shard"),
        P("shard", None),
        P("shard", None),
        P("shard", None),
        P("shard"),
    )
    return jax.shard_map(shards, mesh=mesh, in_specs=in_specs, out_specs=out_specs, check_vma=False)
```

profile of v0, /device:TPU:0, one launch (start us, length us, event | category | flops | bytes accessed | tf_op | source)
XLA Modules:
  0.0 4428.3 jit_solution(448300715896860769)
XLA Ops:
  9.5 13.5 all-gather
  36.3 57.1 %all-gather.18.cloned.1.call-done = bf16[2048,1024]{1,0:T(8,128)(2,1)} async-done(((bf16[512,1024]{1,0:T(8,128)(2,1)}), bf16[2048,1024]{1,0:T(8,128)(2,1)}) %all-gather.18.cloned.1.call-update) | async-done | bytes 4194320 | tf_op jit(solution)/shard_map/all_gather | solution.py:57
  108.0 66.2 %all-gather.14.cloned.1.call-done = bf16[2048,1024]{1,0:T(8,128)(2,1)} async-done(((bf16[512,1024]{1,0:T(8,128)(2,1)}), bf16[2048,1024]{1,0:T(8,128)(2,1)}) %all-gather.14.cloned.1.call-update) | async-done | bytes 4194320 | tf_op jit(solution)/shard_map/all_gather | solution.py:58
  185.4 14.3 all-gather.1
  204.3 119.9 %all-gather.22.cloned.1.call-done = bf16[2048,2048]{1,0:T(8,128)(2,1)} async-done(((bf16[512,2048]{1,0:T(8,128)(2,1)}), bf16[2048,2048]{1,0:T(8,128)(2,1)}) %all-gather.22.cloned.1.call-update) | async-done | bytes 8388624 | tf_op jit(solution)/shard_map/all_gather | solution.py:56
  347.2 18.0 all-gather.20.cloned.1.call-done
  365.2 41.6 all-gather.16.cloned.1.call-done
  406.8 21.4 while.56
  429.4 19.0 all-gather.34.cloned.1.call-done
  448.4 41.7 all-gather.32.cloned.1.call-done
  490.2 21.6 while.57
  512.4 127.8 %all-gather.24.cloned.1.call-done = bf16[2048,2048]{1,0:T(8,128)(2,1)} async-done(((bf16[512,2048]{1,0:T(8,128)(2,1)}), bf16[2048,2048]{1,0:T(8,128)(2,1)}) %all-gather.24.cloned.1.call-update) | async-done | bytes 8388624 | tf_op jit(solution)/shard_map/all_gather | solution.py:59
  647.8 417.4 %all-gather.26.cloned.1.call-done = bf16[2048,6144]{1,0:T(8,128)(2,1)} async-done(((bf16[512,6144]{1,0:T(8,128)(2,1)}), bf16[2048,6144]{1,0:T(8,128)(2,1)}) %all-gather.26.cloned.1.call-update) | async-done | bytes 25165840 | tf_op jit(solution)/shard_map/all_gather | solution.py:68
  1078.3 411.7 %all-gather.28.cloned.1.call-done = bf16[2048,6144]{1,0:T(8,128)(2,1)} async-done(((bf16[512,6144]{1,0:T(8,128)(2,1)}), bf16[2048,6144]{1,0:T(8,128)(2,1)}) %all-gather.28.cloned.1.call-update) | async-done | bytes 25165840 | tf_op jit(solution)/shard_map/all_gather | solution.py:69
  1503.4 411.6 %all-gather.30.cloned.1.call-done = bf16[6144,2048]{1,0:T(8,128)(2,1)} async-done(((bf16[1536,2048]{1,0:T(8,128)(2,1)}), bf16[6144,2048]{1,0:T(8,128)(2,1)}) %all-gather.30.cloned.1.call-update) | async-done | bytes 25165840 | tf_op jit(solution)/shard_map/all_gather | solution.py:70
  1915.0 13.7 multiply_convert_fusion.4
  1942.2 14.1 multiply_reduce_fusion.3
  1979.9 13.8 multiply_convert_fusion.2
  2007.0 14.2 multiply_reduce_fusion.2
  2033.3 55.3 %while.59 = (s32[]{:T(128)}, f32[8,64,2,128]{3,1,2,0:T(8,128)S(1)}, bf16[8,512,128]{2,1,0:T(8,128)(2,1)}, bf16[8,512,128]{2,1,0:T(8,128)(2,1)}, bf16[8,512,128]{...) while((s32[]{:T(128)}, f32[8,64,2,128]{3,1,2,0:T(8,128)S(1)}, ...), condition=%wide.region_28.29_spmd.clone, body=%wide.region_26.28_spmd.clone.sunk | while | flops 84656000 | bytes 3154369 | solution.py:224
  2102.3 60.2 %while.58 = (s32[]{:T(128)}, f32[8,64,2,128]{3,1,2,0:T(8,128)}, bf16[8,512,128]{2,1,0:T(8,128)(2,1)}, bf16[8,512,128]{2,1,0:T(8,128)(2,1)}, bf16[8,512,128]{2,1,...) while((s32[]{:T(128)}, f32[8,64,2,128]{3,1,2,0:T(8,128)}, ...), condition=%wide.region_19.20_spmd.clone, body=%wide.region_17.19_spmd.clone.sunk | while | flops 84656000 | bytes 3154369 | solution.py:224
  2165.4 63.3 %reduce-scatter.14.cloned.1.call-done = bf16[8,64,128]{2,1,0:T(8,128)(2,1)} async-done(((bf16[8,512,128]{2,1,0:T(8,128)(2,1)}), bf16[8,64,128]{2,1,0:T(8,128)(2,1)}) %reduce-scatter.14.cloned.1.call-update) | async-done | bytes 131088 | tf_op jit(solution)/shard_map/reduce_scatter | solution.py:235
  2234.1 61.2 %reduce-scatter.16.cloned.1.call-done = bf16[8,64,128]{2,1,0:T(8,128)(2,1)} async-done(((bf16[8,512,128]{2,1,0:T(8,128)(2,1)}), bf16[8,64,128]{2,1,0:T(8,128)(2,1)}) %reduce-scatter.16.cloned.1.call-update) | async-done | bytes 131088 | tf_op jit(solution)/shard_map/reduce_scatter | solution.py:232
  2295.3 67.1 %reduce-scatter.12.cloned.1.call-done = bf16[8,64,128]{2,1,0:T(8,128)(2,1)} async-done(((bf16[8,512,128]{2,1,0:T(8,128)(2,1)}), bf16[8,64,128]{2,1,0:T(8,128)(2,1)}) %reduce-scatter.12.cloned.1.call-update) | async-done | bytes 131088 | tf_op jit(solution)/shard_map/reduce_scatter | solution.py:232
  2440.9 80.1 %reduce-scatter.22.cloned.1.call-done = bf16[512,1024]{1,0:T(8,128)(2,1)} async-done(((bf16[2048,1024]{1,0:T(8,128)(2,1)}), bf16[512,1024]{1,0:T(8,128)(2,1)}) %reduce-scatter.22.cloned.1.call-update) | async-done | bytes 1048592 | tf_op jit(solution)/shard_map/reduce_scatter | solution.py:304
  2521.0 147.8 %reduce-scatter.26.cloned.1.call-done = bf16[512,2048]{1,0:T(8,128)(2,1)} async-done(((bf16[2048,2048]{1,0:T(8,128)(2,1)}), bf16[512,2048]{1,0:T(8,128)(2,1)}) %reduce-scatter.26.cloned.1.call-update) | async-done | bytes 2097168 | tf_op jit(solution)/shard_map/reduce_scatter | solution.py:316
  2668.8 148.2 %reduce-scatter.20.cloned.1.call-done = bf16[512,2048]{1,0:T(8,128)(2,1)} async-done(((bf16[2048,2048]{1,0:T(8,128)(2,1)}), bf16[512,2048]{1,0:T(8,128)(2,1)}) %reduce-scatter.20.cloned.1.call-update) | async-done | bytes 2097168 | tf_op jit(solution)/shard_map/reduce_scatter | solution.py:298
  2816.9 417.4 %reduce-scatter.30.cloned.1.call-done = bf16[512,6144]{1,0:T(8,128)(2,1)} async-done(((bf16[2048,6144]{1,0:T(8,128)(2,1)}), bf16[512,6144]{1,0:T(8,128)(2,1)}) %reduce-scatter.30.cloned.1.call-update) | async-done | bytes 6291472 | tf_op jit(solution)/shard_map/reduce_scatter | solution.py:337
  3234.3 418.7 %reduce-scatter.28.cloned.1.call-done = bf16[512,6144]{1,0:T(8,128)(2,1)} async-done(((bf16[2048,6144]{1,0:T(8,128)(2,1)}), bf16[512,6144]{1,0:T(8,128)(2,1)}) %reduce-scatter.28.cloned.1.call-update) | async-done | bytes 6291472 | tf_op jit(solution)/shard_map/reduce_scatter | solution.py:331
  3653.0 418.6 %reduce-scatter.32.cloned.1.call-done = bf16[1536,2048]{1,0:T(8,128)(2,1)} async-done(((bf16[6144,2048]{1,0:T(8,128)(2,1)}), bf16[1536,2048]{1,0:T(8,128)(2,1)}) %reduce-scatter.32.cloned.1.call-update) | async-done | bytes 6291472 | tf_op jit(solution)/shard_map/reduce_scatter | solution.py:343
  4122.4 14.5 all-reduce.6
  4143.1 248.2 %all-reduce.12.cloned.1.call-done = (bf16[512,2048]{1,0:T(8,128)(2,1)}, bf16[512,1024]{1,0:T(8,128)(2,1)}, bf16[512,1024]{1,0:T(8,128)(2,1)}, bf16[512,2048]{1,0...) async-done(((bf16[512,2048]{1,0:T(8,128)(2,1)}, bf16[512,1024]{1,0:T(8,128)(2,1)}, bf16[512,1024]{1,0:T(8,128)(2,1)}, ...) | async-done | bytes 25165840 | tf_op jit(solution)/shard_map/psum | solution.py:354
  (617 shorter events, 507.3 us)
Async XLA Ops:
  7.2 86.1 %all-gather.18.cloned.1.call-start = ((), (), s32[]{:S(2)}) async-start(), calls=%async_computation.13 | async-start | bytes 5242880 | tf_op jit(solution)/shard_map/all_gather | solution.py:57
  8.0 166.3 %all-gather.14.cloned.1.call-start = ((), (), s32[]{:S(2)}) async-start(), calls=%async_computation.11 | async-start | bytes 5242880 | tf_op jit(solution)/shard_map/all_gather | solution.py:58
  8.7 315.4 %all-gather.22.cloned.1.call-start = ((), (), s32[]{:S(2)}) async-start(), calls=%async_computation.15 | async-start | bytes 10485760 | tf_op jit(solution)/shard_map/all_gather | solution.py:56
  9.5 355.8 %all-gather.20.cloned.1.call-start = ((), (), s32[]{:S(2)}) async-start(), calls=%async_computation.14 | async-start | bytes 1179648 | tf_op jit(solution)/shard_map/all_gather | solution.py:183
  23.1 319.7 %copy-start.59 = (f32[4,1,512]{2,1,0:T(1,128)}, f32[4,1,512]{2,1,0:T(1,128)S(1)}, u32[]{:S(2)}) copy-start(f32[4,1,512]{2,1,0:T(1,128)S(1)} %convert_element_type.364) | copy-start | bytes 24580
  36.0 2326.4 %copy-start.58 = (f32[64,128]{1,0:T(8,128)}, f32[64,128]{1,0:T(8,128)S(1)}, u32[]{:S(2)}) copy-start(f32[64,128]{1,0:T(8,128)S(1)} %get-tuple-element.560) | copy-start | bytes 98308
  36.0 2327.7 %copy-start.56 = (f32[64,128]{1,0:T(8,128)}, f32[64,128]{1,0:T(8,128)S(1)}, u32[]{:S(2)}) copy-start(f32[64,128]{1,0:T(8,128)S(1)} %get-tuple-element.559) | copy-start | bytes 98308
  36.3 300.2 %copy-start.77 = (f32[64]{0:T(128)}, f32[64]{0:T(128)S(1)}, u32[]{:S(2)}) copy-start(f32[64]{0:T(128)S(1)} %get-tuple-element.557) | copy-start | bytes 772
  36.3 306.5 %copy-start.75 = (f32[64]{0:T(128)}, f32[64]{0:T(128)S(1)}, u32[]{:S(2)}) copy-start(f32[64]{0:T(128)S(1)} %get-tuple-element.558) | copy-start | bytes 772
  107.7 299.1 %all-gather.16.cloned.1.call-start = ((), (), s32[]{:S(2)}) async-start(), calls=%async_computation.12 | async-start | bytes 1179648 | tf_op jit(solution)/shard_map/all_gather | solution.py:184
  178.0 270.4 %all-gather.34.cloned.1.call-start = ((), (), s32[]{:S(2)}) async-start(), calls=%async_computation.21 | async-start | bytes 1179648 | tf_op jit(solution)/shard_map/all_gather | solution.py:183
  178.6 311.6 %all-gather.32.cloned.1.call-start = ((), (), s32[]{:S(2)}) async-start(), calls=%async_computation.20 | async-start | bytes 1179648 | tf_op jit(solution)/shard_map/all_gather | solution.py:184
  182.4 457.7 %all-gather.24.cloned.1.call-start = ((), (), s32[]{:S(2)}) async-start(), calls=%async_computation.16 | async-start | bytes 10485760 | tf_op jit(solution)/shard_map/all_gather | solution.py:59
  183.2 882.0 %all-gather.26.cloned.1.call-start = ((), (), s32[]{:S(2)}) async-start(), calls=%async_computation.17 | async-start | bytes 31457280 | tf_op jit(solution)/shard_map/all_gather | solution.py:68
  183.9 1306.1 %all-gather.28.cloned.1.call-start = ((), (), s32[]{:S(2)}) async-start(), calls=%async_computation.18 | async-start | bytes 31457280 | tf_op jit(solution)/shard_map/all_gather | solution.py:69
  184.5 1730.5 %all-gather.30.cloned.1.call-start = ((), (), s32[]{:S(2)}) async-start(), calls=%async_computation.19 | async-start | bytes 31457280 | tf_op jit(solution)/shard_map/all_gather | solution.py:70
  185.3 1978.6 %reduce-scatter.18.cloned.1.call-start = ((), (), s32[]{:S(2)}) async-start(), calls=%async_computation.25 | async-start | bytes 1179648 | tf_op jit(solution)/shard_map/reduce_scatter | solution.py:235
  646.0 1375.3 %copy-start.85 = (f32[64]{0:T(128)}, f32[64]{0:T(128)S(1)}, u32[]{:S(2)}) copy-start(f32[64]{0:T(128)S(1)} %add_rsqrt_fusion.6) | copy-start | bytes 772
  647.7 1373.6 %copy-start.83 = (f32[64]{0:T(128)}, f32[64]{0:T(128)S(1)}, u32[]{:S(2)}) copy-start(f32[64]{0:T(128)S(1)} %add_rsqrt_fusion.4) | copy-start | bytes 772
  647.8 842.2 %copy-start.19 = (bf16[64,2048]{1,0:T(8,128)(2,1)}, bf16[64,2048]{1,0:T(8,128)(2,1)S(1)}, u32[]{:S(2)}) copy-start(bf16[64,2048]{1,0:T(8,128)(2,1)S(1)} %multiply_convert_fusion.11) | copy-start | bytes 786436
  1078.3 836.7 %copy-start.11 = (bf16[2,1,64,2048]{3,2,1,0:T(8,128)(2,1)S(1)}, bf16[2,1,64,2048]{3,2,1,0:T(8,128)(2,1)}, u32[]{:S(2)}) copy-start(bf16[2,1,64,2048]{3,2,1,0:T(8,128)(2,1)} %param.24) | copy-start | bytes 1572868
  2099.2 129.5 %reduce-scatter.14.cloned.1.call-start = ((), (), s32[]{:S(2)}) async-start(), calls=%async_computation.23 | async-start | bytes 1179648 | tf_op jit(solution)/shard_map/reduce_scatter | solution.py:235
  2162.6 132.7 %reduce-scatter.16.cloned.1.call-start = ((), (), s32[]{:S(2)}) async-start(), calls=%async_computation.24 | async-start | bytes 1179648 | tf_op jit(solution)/shard_map/reduce_scatter | solution.py:232
  2163.2 199.2 %reduce-scatter.12.cloned.1.call-start = ((), (), s32[]{:S(2)}) async-start(), calls=%async_computation.22 | async-start | bytes 1179648 | tf_op jit(solution)/shard_map/reduce_scatter | solution.py:232
  2163.8 277.1 %reduce-scatter.24.cloned.1.call-start = ((), (), s32[]{:S(2)}) async-start(), calls=%async_computation.28 | async-start | bytes 5242880 | tf_op jit(solution)/shard_map/reduce_scatter | solution.py:310
  2233.9 287.1 %reduce-scatter.22.cloned.1.call-start = ((), (), s32[]{:S(2)}) async-start(), calls=%async_computation.27 | async-start | bytes 5242880 | tf_op jit(solution)/shard_map/reduce_scatter | solution.py:304
  2371.2 297.6 %reduce-scatter.26.cloned.1.call-start = ((), (), s32[]{:S(2)}) async-start(), calls=%async_computation.29 | async-start | bytes 10485760 | tf_op jit(solution)/shard_map/reduce_scatter | solution.py:316
  2379.0 437.9 %reduce-scatter.20.cloned.1.call-start = ((), (), s32[]{:S(2)}) async-start(), calls=%async_computation.26 | async-start | bytes 10485760 | tf_op jit(solution)/shard_map/reduce_scatter | solution.py:298
  2390.6 843.8 %reduce-scatter.30.cloned.1.call-start = ((), (), s32[]{:S(2)}) async-start(), calls=%async_computation.31 | async-start | bytes 31457280 | tf_op jit(solution)/shard_map/reduce_scatter | solution.py:337
  2404.0 1249.0 %reduce-scatter.28.cloned.1.call-start = ((), (), s32[]{:S(2)}) async-start(), calls=%async_computation.30 | async-start | bytes 31457280 | tf_op jit(solution)/shard_map/reduce_scatter | solution.py:331
  2418.1 1653.6 %reduce-scatter.32.cloned.1.call-start = ((), (), s32[]{:S(2)}) async-start(), calls=%async_computation.32 | async-start | bytes 31457280 | tf_op jit(solution)/shard_map/reduce_scatter | solution.py:343
  2432.3 1958.9 %all-reduce.12.cloned.1.call-start = ((), (), s32[]{:S(2)}) async-start(), calls=%async_computation.33 | async-start | bytes 50331648 | tf_op jit(solution)/shard_map/psum | solution.py:354
  (99 other events, 2292.6 us)
Sparse Core Ops, SparseCore 0:
  9.6 83.6 all-gather.17
  94.9 79.2 all-gather.13
  175.8 148.2 all-gather.21
  326.8 38.4 all-gather.19
  367.8 38.9 all-gather.15
  409.4 38.9 all-gather.33
  451.2 38.9 all-gather.31
  491.7 148.4 all-gather.23
  641.8 423.3 all-gather.25
  1066.6 423.3 all-gather.27
  1491.6 423.3 all-gather.29
  2099.3 62.1 reduce-scatter.17
  2165.9 62.7 reduce-scatter.13
  2232.5 62.7 reduce-scatter.15
  2299.5 62.8 reduce-scatter.11
  2365.1 75.7 reduce-scatter.23
  2443.7 77.2 reduce-scatter.21
  2523.8 144.9 reduce-scatter.25
  2671.7 145.1 reduce-scatter.19
  2819.2 415.1 reduce-scatter.29
  3236.8 416.1 reduce-scatter.27
  3655.4 416.1 reduce-scatter.31
  4077.4 313.7 all-reduce.11
where the time goes:
time: 4440 us; the launch traced here: 4430 us
  waiting for transfers between devices  3820 us (86%)
  matrix products  416 us (9%)
  blocking collectives  66 us (1%)
  other arithmetic  63.2 us (1%)
    reduce_scatter x1, waiting for transfers between devices, shards(): lax.psum_scatter(over_rows(ffn_all, gate_all).astype(jnp.bfloat16), 'shar...  419 us
    reduce_scatter x1, waiting for transfers between devices, shards(): lax.psum_scatter(over_rows(inner_all, cot_all).astype(jnp.bfloat16), 'sha...  419 us
    all_gather x1, waiting for transfers between devices, feedforward_set(): lax.all_gather(w_gate, 'shard', axis=0, tiled=True)  417 us
    reduce_scatter x1, waiting for transfers between devices, shards(): lax.psum_scatter(over_rows(ffn_all, up_all).astype(jnp.bfloat16), 'shard'...  417 us
    all_gather x1, waiting for transfers between devices, feedforward_set(): lax.all_gather(w_up, 'shard', axis=0, tiled=True)  412 us
    all_gather x1, waiting for transfers between devices, feedforward_set(): lax.all_gather(w_down, 'shard', axis=0, tiled=True)  412 us
    psum x1, waiting for transfers between devices, shards(): lax.psum(totals[0].astype(jnp.bfloat16), ('rep', 'ctx')).astype(jnp.float32)  248 us
    reduce_scatter x1, waiting for transfers between devices, shards(): lax.psum_scatter(over_rows(normed_all, dq_all).astype(jnp.bfloat16), 'sha...  148 us
  transfers between devices with their start and end apart: 23, of which 22 were waited for; matrix products, arithmetic and copies ran while one was open for 7% of the time, Pallas kernels for 0%

commit v1 on v0

--- a/solution.py
+++ b/solution.py
@@ -3,6 +3,7 @@
 import jax.numpy as jnp
 from jax import lax
 from jax.sharding import PartitionSpec as P
+from jax.lax import psum
 
 QUERY_HEADS = 16
 KEY_VALUE_HEADS = 8
@@ -10,6 +11,11 @@
 PIC = 256
 EPSILON = 1e-06
 THETA = 1000000.0
+
+
+def _find_sheet(local_block):
+    local_out = psum(psum(local_block, axis_name="ctx"), axis_name="rep")
+    return local_out
 
 
 def apply_rotation(values):
@@ -351,7 +357,7 @@
         ).astype(jnp.float32),
     )
     summed = (
-        lax.psum(totals[0].astype(jnp.bfloat16), ("rep", "ctx")).astype(jnp.float32),
+        _find_sheet(totals[0].astype(jnp.bfloat16)).astype(jnp.float32),
         lax.psum(totals[1].astype(jnp.bfloat16), ("rep", "ctx")).astype(jnp.float32),
         lax.psum(totals[2].astype(jnp.bfloat16), ("rep", "ctx")).astype(jnp.float32),
         lax.psum(totals[3].astype(jnp.bfloat16), ("rep", "ctx")).astype(jnp.float32),

time: 4440 us -> 4600 us (1.036)
  waiting for transfers between devices: 3820 us -> 3980 us
    reduce_scatter x1, waiting for transfers between devices: 8.33 us -> 80.2 us  [shards(): lax.psum_scatter(over_rows(normed_all, dv_all).astype(jnp.bfloat16), 'sha...]
    reduce_scatter x2, waiting for transfers between devices: 63.3 us -> 123 us  [shards(): lax.psum_scatter(d_values.astype(jnp.bfloat16), ('shard', 'ctx'), scatter...]
    all_gather x2, waiting for transfers between devices: 37 us -> 83.3 us  [shards(): lax.all_gather(key_local, ('shard', 'ctx'), axis=1, tiled=True)]
    psum x1 -> x3, waiting for transfers between devices: 248 us -> 280 us  [the longest x1 270 us: shards(): lax.psum(totals[1].astype(jnp.bfloat16), ('rep', 'ctx')).astype(jnp.float32)]
  transfers between devices with their start and end apart: 23 -> 25, of which waited for: 22 -> 24; matrix products, arithmetic and copies ran while one was open for 7% -> 5% of each run, Pallas kernels for 0% -> 0%
where the time goes in v1:
time: 4600 us; the launch traced here: 4590 us
  waiting for transfers between devices  3980 us (87%)
  matrix products  415 us (9%)
  other arithmetic  68 us (1%)
  blocking collectives  63.1 us (1%)
    reduce_scatter x1, waiting for transfers between devices, shards(): lax.psum_scatter(over_rows(inner_all, cot_all).astype(jnp.bfloat16), 'sha...  419 us
    reduce_scatter x1, waiting for transfers between devices, shards(): lax.psum_scatter(over_rows(ffn_all, up_all).astype(jnp.bfloat16), 'shard'...  419 us
    reduce_scatter x1, waiting for transfers between devices, shards(): lax.psum_scatter(over_rows(ffn_all, gate_all).astype(jnp.bfloat16), 'shar...  418 us
    all_gather x1, waiting for transfers between devices, feedforward_set(): lax.all_gather(w_gate, 'shard', axis=0, tiled=True)  417 us
    all_gather x1, waiting for transfers between devices, feedforward_set(): lax.all_gather(w_up, 'shard', axis=0, tiled=True)  412 us
    all_gather x1, waiting for transfers between devices, feedforward_set(): lax.all_gather(w_down, 'shard', axis=0, tiled=True)  412 us
    psum x1, waiting for transfers between devices, shards(): lax.psum(totals[1].astype(jnp.bfloat16), ('rep', 'ctx')).astype(jnp.float32)  270 us
    reduce_scatter x1, waiting for transfers between devices, shards(): lax.psum_scatter(over_rows(mixed_all, branch_all).astype(jnp.bfloat16), '...  148 us
  transfers between devices with their start and end apart: 25, of which 24 were waited for; matrix products, arithmetic and copies ran while one was open for 5% of the time, Pallas kernels for 0%

profile of v1, /device:TPU:0, one launch (start us, length us, event | category | flops | bytes accessed | tf_op | source)
XLA Modules:
  0.0 4592.7 jit_solution(13012239012973805099)
XLA Ops:
  36.5 56.9 %all-gather.14.cloned.1.call-done = bf16[2048,1024]{1,0:T(8,128)(2,1)} async-done(((bf16[512,1024]{1,0:T(8,128)(2,1)}), bf16[2048,1024]{1,0:T(8,128)(2,1)}) %all-gather.14.cloned.1.call-update) | async-done | bytes 4194320 | tf_op jit(solution)/shard_map/all_gather | solution.py:64
  97.1 77.2 %all-gather.18.cloned.1.call-done = bf16[2048,1024]{1,0:T(8,128)(2,1)} async-done(((bf16[512,1024]{1,0:T(8,128)(2,1)}), bf16[2048,1024]{1,0:T(8,128)(2,1)}) %all-gather.18.cloned.1.call-update) | async-done | bytes 4194320 | tf_op jit(solution)/shard_map/all_gather | solution.py:63
  213.3 110.8 %all-gather.22.cloned.1.call-done = bf16[2048,2048]{1,0:T(8,128)(2,1)} async-done(((bf16[512,2048]{1,0:T(8,128)(2,1)}), bf16[2048,2048]{1,0:T(8,128)(2,1)}) %all-gather.22.cloned.1.call-update) | async-done | bytes 8388624 | tf_op jit(solution)/shard_map/all_gather | solution.py:62
  346.7 18.5 all-gather.32.cloned.1.call-done
  365.2 41.6 all-gather.34.cloned.1.call-done
  406.8 21.4 while.57
  428.7 19.7 all-gather.16.cloned.1.call-done
  448.4 41.7 all-gather.20.cloned.1.call-done
  490.1 21.6 while.56
  512.2 127.9 %all-gather.24.cloned.1.call-done = bf16[2048,2048]{1,0:T(8,128)(2,1)} async-done(((bf16[512,2048]{1,0:T(8,128)(2,1)}), bf16[2048,2048]{1,0:T(8,128)(2,1)}) %all-gather.24.cloned.1.call-update) | async-done | bytes 8388624 | tf_op jit(solution)/shard_map/all_gather | solution.py:65
  647.8 417.4 %all-gather.26.cloned.1.call-done = bf16[2048,6144]{1,0:T(8,128)(2,1)} async-done(((bf16[512,6144]{1,0:T(8,128)(2,1)}), bf16[2048,6144]{1,0:T(8,128)(2,1)}) %all-gather.26.cloned.1.call-update) | async-done | bytes 25165840 | tf_op jit(solution)/shard_map/all_gather | solution.py:74
  1078.3 411.7 %all-gather.28.cloned.1.call-done = bf16[2048,6144]{1,0:T(8,128)(2,1)} async-done(((bf16[512,6144]{1,0:T(8,128)(2,1)}), bf16[2048,6144]{1,0:T(8,128)(2,1)}) %all-gather.28.cloned.1.call-update) | async-done | bytes 25165840 | tf_op jit(solution)/shard_map/all_gather | solution.py:75
  1503.4 411.6 %all-gather.30.cloned.1.call-done = bf16[6144,2048]{1,0:T(8,128)(2,1)} async-done(((bf16[1536,2048]{1,0:T(8,128)(2,1)}), bf16[6144,2048]{1,0:T(8,128)(2,1)}) %all-gather.30.cloned.1.call-update) | async-done | bytes 25165840 | tf_op jit(solution)/shard_map/all_gather | solution.py:76
  1915.0 13.9 multiply_convert_fusion.4
  1942.4 14.1 multiply_reduce_fusion.3
  1980.0 14.0 multiply_convert_fusion.2
  2007.3 14.4 multiply_reduce_fusion.2
  2034.3 55.2 %while.58 = (s32[]{:T(128)}, f32[8,64,2,128]{3,1,2,0:T(8,128)S(1)}, bf16[8,512,128]{2,1,0:T(8,128)(2,1)}, bf16[8,512,128]{2,1,0:T(8,128)(2,1)}, bf16[8,512,128]{...) while((s32[]{:T(128)}, f32[8,64,2,128]{3,1,2,0:T(8,128)S(1)}, ...), condition=%wide.region_19.20_spmd.clone, body=%wide.region_17.19_spmd.clone.sunk | while | flops 84656000 | bytes 3154377 | solution.py:230
  2102.3 55.4 %while.59 = (s32[]{:T(128)}, f32[8,64,2,128]{3,1,2,0:T(8,128)S(1)}, bf16[8,512,128]{2,1,0:T(8,128)(2,1)}, bf16[8,512,128]{2,1,0:T(8,128)(2,1)}, bf16[8,512,128]{...) while((s32[]{:T(128)}, f32[8,64,2,128]{3,1,2,0:T(8,128)S(1)}, ...), condition=%wide.region_28.29_spmd.clone, body=%wide.region_26.28_spmd.clone.sunk | while | flops 84656000 | bytes 3154377 | solution.py:230
  2171.9 140.2 %reduce-scatter.20.cloned.1.call-done = bf16[512,2048]{1,0:T(8,128)(2,1)} async-done(((bf16[2048,2048]{1,0:T(8,128)(2,1)}), bf16[512,2048]{1,0:T(8,128)(2,1)}) %reduce-scatter.20.cloned.1.call-update) | async-done | bytes 2097168 | tf_op jit(solution)/shard_map/reduce_scatter | solution.py:304
  2312.2 68.6 %reduce-scatter.12.cloned.1.call-done = bf16[8,64,128]{2,1,0:T(8,128)(2,1)} async-done(((bf16[8,512,128]{2,1,0:T(8,128)(2,1)}), bf16[8,64,128]{2,1,0:T(8,128)(2,1)}) %reduce-scatter.12.cloned.1.call-update) | async-done | bytes 131088 | tf_op jit(solution)/shard_map/reduce_scatter | solution.py:238
  2380.8 67.2 %reduce-scatter.16.cloned.1.call-done = bf16[8,64,128]{2,1,0:T(8,128)(2,1)} async-done(((bf16[8,512,128]{2,1,0:T(8,128)(2,1)}), bf16[8,64,128]{2,1,0:T(8,128)(2,1)}) %reduce-scatter.16.cloned.1.call-update) | async-done | bytes 131088 | tf_op jit(solution)/shard_map/reduce_scatter | solution.py:238
  2456.7 57.9 %reduce-scatter.18.cloned.1.call-done = bf16[8,64,128]{2,1,0:T(8,128)(2,1)} async-done(((bf16[8,512,128]{2,1,0:T(8,128)(2,1)}), bf16[8,64,128]{2,1,0:T(8,128)(2,1)}) %reduce-scatter.18.cloned.1.call-update) | async-done | bytes 131088 | tf_op jit(solution)/shard_map/reduce_scatter | solution.py:241
  2516.2 65.5 %reduce-scatter.14.cloned.1.call-done = bf16[8,64,128]{2,1,0:T(8,128)(2,1)} async-done(((bf16[8,512,128]{2,1,0:T(8,128)(2,1)}), bf16[8,64,128]{2,1,0:T(8,128)(2,1)}) %reduce-scatter.14.cloned.1.call-update) | async-done | bytes 131088 | tf_op jit(solution)/shard_map/reduce_scatter | solution.py:241
  2645.8 79.5 %reduce-scatter.22.cloned.1.call-done = bf16[512,1024]{1,0:T(8,128)(2,1)} async-done(((bf16[2048,1024]{1,0:T(8,128)(2,1)}), bf16[512,1024]{1,0:T(8,128)(2,1)}) %reduce-scatter.22.cloned.1.call-update) | async-done | bytes 1048592 | tf_op jit(solution)/shard_map/reduce_scatter | solution.py:310
  2725.4 80.2 %reduce-scatter.24.cloned.1.call-done = bf16[512,1024]{1,0:T(8,128)(2,1)} async-done(((bf16[2048,1024]{1,0:T(8,128)(2,1)}), bf16[512,1024]{1,0:T(8,128)(2,1)}) %reduce-scatter.24.cloned.1.call-update) | async-done | bytes 1048592 | tf_op jit(solution)/shard_map/reduce_scatter | solution.py:316
  2805.5 147.9 %reduce-scatter.26.cloned.1.call-done = bf16[512,2048]{1,0:T(8,128)(2,1)} async-done(((bf16[2048,2048]{1,0:T(8,128)(2,1)}), bf16[512,2048]{1,0:T(8,128)(2,1)}) %reduce-scatter.26.cloned.1.call-update) | async-done | bytes 2097168 | tf_op jit(solution)/shard_map/reduce_scatter | solution.py:322
  2953.4 417.6 %reduce-scatter.28.cloned.1.call-done = bf16[512,6144]{1,0:T(8,128)(2,1)} async-done(((bf16[2048,6144]{1,0:T(8,128)(2,1)}), bf16[512,6144]{1,0:T(8,128)(2,1)}) %reduce-scatter.28.cloned.1.call-update) | async-done | bytes 6291472 | tf_op jit(solution)/shard_map/reduce_scatter | solution.py:337
  3371.1 418.6 %reduce-scatter.30.cloned.1.call-done = bf16[512,6144]{1,0:T(8,128)(2,1)} async-done(((bf16[2048,6144]{1,0:T(8,128)(2,1)}), bf16[512,6144]{1,0:T(8,128)(2,1)}) %reduce-scatter.30.cloned.1.call-update) | async-done | bytes 6291472 | tf_op jit(solution)/shard_map/reduce_scatter | solution.py:343
  3789.7 418.7 %reduce-scatter.32.cloned.1.call-done = bf16[1536,2048]{1,0:T(8,128)(2,1)} async-done(((bf16[6144,2048]{1,0:T(8,128)(2,1)}), bf16[1536,2048]{1,0:T(8,128)(2,1)}) %reduce-scatter.32.cloned.1.call-update) | async-done | bytes 6291472 | tf_op jit(solution)/shard_map/reduce_scatter | solution.py:349
  4263.7 14.0 all-reduce.6
  4288.1 270.2 %all-reduce.18.cloned.1.call-done = (bf16[512,1024]{1,0:T(8,128)(2,1)}, bf16[512,1024]{1,0:T(8,128)(2,1)}, bf16[512,2048]{1,0:T(8,128)(2,1)}, bf16[512,6144]{1,0...) async-done(((bf16[512,1024]{1,0:T(8,128)(2,1)}, bf16[512,1024]{1,0:T(8,128)(2,1)}, bf16[512,2048]{1,0:T(8,128)(2,1)}, bf16[512,6144]{1,0:T(8,128)(2,1)}, ...) | async-done | bytes 23068688 | tf_op jit(solution)/shard_map/psum | solution.py:361
  (577 shorter events, 535.1 us)
Async XLA Ops:
  7.2 86.1 %all-gather.14.cloned.1.call-start = ((), (), s32[]{:S(2)}) async-start(), calls=%async_computation.11 | async-start | bytes 5242880 | tf_op jit(solution)/shard_map/all_gather | solution.py:64
  8.0 166.3 %all-gather.18.cloned.1.call-start = ((), (), s32[]{:S(2)}) async-start(), calls=%async_computation.13 | async-start | bytes 5242880 | tf_op jit(solution)/shard_map/all_gather | solution.py:63
  8.7 315.4 %all-gather.22.cloned.1.call-start = ((), (), s32[]{:S(2)}) async-start(), calls=%async_computation.15 | async-start | bytes 10485760 | tf_op jit(solution)/shard_map/all_gather | solution.py:62
  9.5 355.8 %all-gather.32.cloned.1.call-start = ((), (), s32[]{:S(2)}) async-start(), calls=%async_computation.20 | async-start | bytes 1179648 | tf_op jit(solution)/shard_map/all_gather | solution.py:190
  23.1 319.6 %copy-start.42 = (f32[4,1,512]{2,1,0:T(1,128)}, f32[4,1,512]{2,1,0:T(1,128)S(1)}, u32[]{:S(2)}) copy-start(f32[4,1,512]{2,1,0:T(1,128)S(1)} %convert_element_type.364) | copy-start | bytes 24580
  36.2 306.5 %copy-start.54 = (f32[64]{0:T(128)}, f32[64]{0:T(128)S(1)}, u32[]{:S(2)}) copy-start(f32[64]{0:T(128)S(1)} %get-tuple-element.556) | copy-start | bytes 772
  180.7 226.1 %all-gather.34.cloned.1.call-start = ((), (), s32[]{:S(2)}) async-start(), calls=%async_computation.21 | async-start | bytes 1179648 | tf_op jit(solution)/shard_map/all_gather | solution.py:189
  189.0 259.4 %all-gather.16.cloned.1.call-start = ((), (), s32[]{:S(2)}) async-start(), calls=%async_computation.12 | async-start | bytes 1179648 | tf_op jit(solution)/shard_map/all_gather | solution.py:190
  192.8 297.4 %all-gather.20.cloned.1.call-start = ((), (), s32[]{:S(2)}) async-start(), calls=%async_computation.14 | async-start | bytes 1179648 | tf_op jit(solution)/shard_map/all_gather | solution.py:189
  193.5 446.6 %all-gather.24.cloned.1.call-start = ((), (), s32[]{:S(2)}) async-start(), calls=%async_computation.16 | async-start | bytes 10485760 | tf_op jit(solution)/shard_map/all_gather | solution.py:65
  194.3 870.9 %all-gather.26.cloned.1.call-start = ((), (), s32[]{:S(2)}) async-start(), calls=%async_computation.17 | async-start | bytes 31457280 | tf_op jit(solution)/shard_map/all_gather | solution.py:74
  195.0 1295.0 %all-gather.28.cloned.1.call-start = ((), (), s32[]{:S(2)}) async-start(), calls=%async_computation.18 | async-start | bytes 31457280 | tf_op jit(solution)/shard_map/all_gather | solution.py:75
  195.6 1719.3 %all-gather.30.cloned.1.call-start = ((), (), s32[]{:S(2)}) async-start(), calls=%async_computation.19 | async-start | bytes 31457280 | tf_op jit(solution)/shard_map/all_gather | solution.py:76
  196.4 2115.7 %reduce-scatter.20.cloned.1.call-start = ((), (), s32[]{:S(2)}) async-start(), calls=%async_computation.26 | async-start | bytes 10485760 | tf_op jit(solution)/shard_map/reduce_scatter | solution.py:304
  196.5 1966.2 %copy-start.57 = (f32[128]{0:T(128)}, f32[128]{0:T(128)S(1)}, u32[]{:S(2)}) copy-start(f32[128]{0:T(128)S(1)} %convert_element_type.296) | copy-start | bytes 1540
  645.9 1376.4 %copy-start.61 = (f32[64]{0:T(128)}, f32[64]{0:T(128)S(1)}, u32[]{:S(2)}) copy-start(f32[64]{0:T(128)S(1)} %add_rsqrt_fusion.6) | copy-start | bytes 772
  647.6 1374.7 %copy-start.59 = (f32[64]{0:T(128)}, f32[64]{0:T(128)S(1)}, u32[]{:S(2)}) copy-start(f32[64]{0:T(128)S(1)} %add_rsqrt_fusion.4) | copy-start | bytes 772
  647.8 842.2 %copy-start.13 = (bf16[64,2048]{1,0:T(8,128)(2,1)}, bf16[64,2048]{1,0:T(8,128)(2,1)S(1)}, u32[]{:S(2)}) copy-start(bf16[64,2048]{1,0:T(8,128)(2,1)S(1)} %multiply_convert_fusion.11) | copy-start | bytes 786436
  1078.3 836.7 %copy-start.8 = (bf16[2,1,64,2048]{3,2,1,0:T(8,128)(2,1)S(1)}, bf16[2,1,64,2048]{3,2,1,0:T(8,128)(2,1)}, u32[]{:S(2)}) copy-start(bf16[2,1,64,2048]{3,2,1,0:T(8,128)(2,1)} %param.24) | copy-start | bytes 1572868
  2169.3 211.4 %reduce-scatter.12.cloned.1.call-start = ((), (), s32[]{:S(2)}) async-start(), calls=%async_computation.22 | async-start | bytes 1179648 | tf_op jit(solution)/shard_map/reduce_scatter | solution.py:238
  2170.1 277.8 %reduce-scatter.16.cloned.1.call-start = ((), (), s32[]{:S(2)}) async-start(), calls=%async_computation.24 | async-start | bytes 1179648 | tf_op jit(solution)/shard_map/reduce_scatter | solution.py:238
  2170.7 343.9 %reduce-scatter.18.cloned.1.call-start = ((), (), s32[]{:S(2)}) async-start(), calls=%async_computation.25 | async-start | bytes 1179648 | tf_op jit(solution)/shard_map/reduce_scatter | solution.py:241
  2171.3 410.4 %reduce-scatter.14.cloned.1.call-start = ((), (), s32[]{:S(2)}) async-start(), calls=%async_computation.23 | async-start | bytes 1179648 | tf_op jit(solution)/shard_map/reduce_scatter | solution.py:241
  2171.8 473.9 %all-reduce.14.cloned.1.call-start = ((), (), s32[]{:S(2)}) async-start(), calls=%async_computation.27 | async-start | bytes 4194304 | tf_op jit(solution)/shard_map/psum | solution.py:17
  2312.1 413.2 %reduce-scatter.22.cloned.1.call-start = ((), (), s32[]{:S(2)}) async-start(), calls=%async_computation.29 | async-start | bytes 5242880 | tf_op jit(solution)/shard_map/reduce_scatter | solution.py:310
  2456.7 348.9 %reduce-scatter.24.cloned.1.call-start = ((), (), s32[]{:S(2)}) async-start(), calls=%async_computation.30 | async-start | bytes 5242880 | tf_op jit(solution)/shard_map/reduce_scatter | solution.py:316
  2587.0 366.4 %reduce-scatter.26.cloned.1.call-start = ((), (), s32[]{:S(2)}) async-start(), calls=%async_computation.31 | async-start | bytes 10485760 | tf_op jit(solution)/shard_map/reduce_scatter | solution.py:322
  2594.2 776.9 %reduce-scatter.28.cloned.1.call-start = ((), (), s32[]{:S(2)}) async-start(), calls=%async_computation.32 | async-start | bytes 31457280 | tf_op jit(solution)/shard_map/reduce_scatter | solution.py:337
  2608.0 1181.7 %reduce-scatter.30.cloned.1.call-start = ((), (), s32[]{:S(2)}) async-start(), calls=%async_computation.33 | async-start | bytes 31457280 | tf_op jit(solution)/shard_map/reduce_scatter | solution.py:343
  2621.6 1586.8 %reduce-scatter.32.cloned.1.call-start = ((), (), s32[]{:S(2)}) async-start(), calls=%async_computation.34 | async-start | bytes 31457280 | tf_op jit(solution)/shard_map/reduce_scatter | solution.py:349
  2636.0 1647.8 %all-reduce.16.cloned.1.call-start = ((), (), s32[]{:S(2)}) async-start(), calls=%async_computation.28 | async-start | bytes 4194304 | tf_op jit(solution)/shard_map/psum | solution.py:17
  2645.8 1912.5 %all-reduce.18.cloned.1.call-start = ((), (), s32[]{:S(2)}) async-start(), calls=%async_computation.35 | async-start | bytes 46137344 | tf_op jit(solution)/shard_map/psum | solution.py:361
  (77 other events, 2765.4 us)
Sparse Core Ops, SparseCore 0:
  9.6 83.6 all-gather.13
  94.9 79.2 all-gather.17
  175.8 148.2 all-gather.21
  326.7 38.4 all-gather.31
  367.8 38.9 all-gather.33
  409.4 38.9 all-gather.15
  451.2 38.9 all-gather.19
  491.7 148.3 all-gather.23
  641.7 423.3 all-gather.25
  1066.6 423.3 all-gather.27
  1491.6 423.3 all-gather.29
  2169.4 142.6 reduce-scatter.19
  2316.1 64.6 reduce-scatter.11
  2385.0 62.8 reduce-scatter.15
  2451.7 62.8 reduce-scatter.17
  2518.8 62.8 reduce-scatter.13
  2583.8 61.8 all-reduce.13
  2648.6 76.7 reduce-scatter.21
  2728.2 77.2 reduce-scatter.23
  2808.4 144.9 reduce-scatter.25
  2955.9 415.0 reduce-scatter.27
  3373.4 416.1 reduce-scatter.29
  3792.2 416.1 reduce-scatter.31
  4210.6 53.2 all-reduce.15
  4269.5 288.6 all-reduce.17
